TPU v7x, 512 devices: a whole 4x4x16 slice. The times are simulated.
512 devices in a mesh: dp: 2 (over core), ctx: 64 (over x, z), head: 4 (over y).
Axes of the slice: x: 4, y: 4, z: 16, core: 2. Of those that a mesh axis runs over, the one named last changes fastest.
Arguments:
- query: bfloat16 [2, 64, 4, 512, 256], P('dp', 'ctx', 'head'), may hold values from -120 to 120
- key: bfloat16 [2, 8192, 4096], P('dp', 'ctx', 'head'), may hold values from -8 to 8
- value: bfloat16 [2, 8192, 4096], P('dp', 'ctx', 'head'), may hold values from -6 to 6
- grad_out: bfloat16 [2, 64, 4, 512, 256], P('dp', 'ctx', 'head'), may hold values from -6 to 6
- chosen: int32 [2, 16, 32, 3], P('dp', None, 'head'), may hold values from 0 to 15, as said below
- placed: int32 [16], replicated, may hold values from 0 to 15, each once
- sink: float32 [32], P('head'), may hold values from -2 to 6
Outputs:
- attended: bfloat16 [2, 64, 4, 512, 256], P('dp', 'ctx', 'head')
- grad_query: bfloat16 [2, 64, 4, 512, 256], P('dp', 'ctx', 'head')
- grad_key: bfloat16 [2, 8192, 4096], P('dp', 'ctx', 'head')
- grad_value: bfloat16 [2, 8192, 4096], P('dp', 'ctx', 'head')
- grad_sink: float32 [32], replicated
Inputs may be any that keep to these rules, and one draw needn't show every extreme that they name: `chosen`: for each sequence, block b and head, the first min(b, 3) entries are distinct blocks before b; the remaining entries are blocks from b to 15. `placed`: every block is held by exactly one slot.
All inputs are finite; a program needn't handle non-finite values.
Results may differ from a plain program's by a relative error of at most 0.025.
Values may be sent and summed in bfloat16 or wider, within the bound.
No kernel may reach another device: no remote copies, remote signals or barrier semaphores. Data moves between devices by JAX's collectives and lax.ppermute only.
A program may use at most 64 MiB of HBM per device.

v0:
```python
import math
import jax
import jax.numpy as jnp
from jax import lax
from jax.sharding import PartitionSpec as P

HEADS = 32
DH = 128


def inner_rows(left, right):
    return lax.dot_general(
        left, right, (((1,), (1,)), ((), ())), preferred_element_type=jnp.float32
    )


def outer_rows(left, right):
    return lax.dot_general(
        left, right, (((0,), (0,)), ((), ())), preferred_element_type=jnp.float32
    )


def attend_block(query_rows, grad_rows, tiles, usable, sink_logit):
    rows, width = query_rows.shape
    scale = 1.0 / math.sqrt(width)
    keys = tiles[:, :, :width].reshape(-1, width)
    vals = tiles[:, :, width:].reshape(-1, width)
    scores = inner_rows(query_rows, keys) * scale
    cols = tiles.shape[0] * rows
    tile_of = jnp.arange(cols) // rows
    offset = jnp.arange(cols) % rows
    own_ok = offset[None, :] <= jnp.arange(rows)[:, None]
    allowed = jnp.where(tile_of[None, :] == 0, own_ok, usable[tile_of][None, :])
    masked = jnp.where(allowed, scores, -jnp.inf)
    top = jnp.maximum(jnp.max(masked, axis=1), sink_logit)
    expo = jnp.exp(masked - top[:, None])
    sink_part = jnp.exp(sink_logit - top)
    total = sink_part + jnp.sum(expo, axis=1)
    prob = expo / total[:, None]
    weights = prob.astype(jnp.bfloat16)
    attended = jnp.dot(weights, vals, preferred_element_type=jnp.float32).astype(jnp.bfloat16)
    stored = lax.optimization_barrier(attended)
    delta = jnp.sum(grad_rows.astype(jnp.float32) * stored.astype(jnp.float32), axis=1)
    dprob = inner_rows(grad_rows, vals)
    dscore = (prob * (dprob - delta[:, None]) * scale).astype(jnp.bfloat16)
    grad_query = jnp.dot(dscore, keys, preferred_element_type=jnp.float32).astype(jnp.bfloat16)
    grad_keys = outer_rows(dscore, query_rows).astype(jnp.bfloat16)
    grad_vals = outer_rows(weights, grad_rows).astype(jnp.bfloat16)
    tiles_grad = jnp.concatenate([grad_keys, grad_vals], axis=1).reshape(tiles.shape)
    sink_grad = -jnp.sum(sink_part / total * delta)
    return (attended, grad_query, tiles_grad, sink_grad)


def body(query, key, value, grad_out, chosen, placed, sink):
    seqs = query.shape[0]
    block = query.shape[3]
    width = DH
    hpd = query.shape[4] // width
    unit = key.shape[1]
    parts_per = block // unit
    n_ctx = lax.axis_size("ctx")
    nblk = n_ctx // parts_per
    place = lax.axis_index("ctx")
    slot = place // parts_per
    position = place % parts_per
    slots = jnp.arange(nblk, dtype=jnp.int32)
    seq_block = jnp.sum(jnp.where(slots == slot, placed, 0))
    slot_of = jnp.sum(jnp.where(placed[None, :] == slots[:, None], slots[None, :], 0), axis=1)
    mine = lax.dynamic_slice_in_dim(chosen, seq_block, 1, 1)[:, 0]
    mine = lax.dynamic_slice_in_dim(mine, position * hpd, hpd, 1)
    usable_pick = mine < seq_block
    mapped = jnp.sum(jnp.where(mine[..., None] == slots, slot_of, 0), axis=-1)
    mapped = jnp.where(usable_pick, mapped, slot)
    lead = jnp.broadcast_to(slot, mine.shape[:2] + (1,))
    picks = jnp.concatenate([lead, mapped], axis=-1)
    kinds = picks.shape[-1]
    usable = jnp.concatenate([jnp.ones(mine.shape[:2] + (1,), bool), usable_pick], axis=-1)
    sink_mine = lax.dynamic_slice_in_dim(sink, position * hpd, hpd)
    paired = jnp.concatenate(
        [
            key.reshape(seqs, unit, parts_per, hpd, width),
            value.reshape(seqs, unit, parts_per, hpd, width),
        ],
        axis=-1,
    )
    paired = jnp.transpose(paired, (2, 0, 3, 1, 4))
    items = seqs * hpd
    frag = unit * 2 * width // n_ctx
    seq_ix = jnp.arange(seqs, dtype=jnp.int32)[None, :, None, None, None]
    head_ix = jnp.arange(hpd, dtype=jnp.int32)[None, None, :, None, None]
    spread = jnp.transpose(paired.reshape(parts_per, seqs, hpd, n_ctx, frag), (3, 0, 1, 2, 4))
    held = lax.all_to_all(spread, "ctx", split_axis=0, concat_axis=0, tiled=True)
    held = jnp.transpose(held, (2, 3, 0, 1, 4)).reshape(seqs, hpd, n_ctx * parts_per, frag)
    match_block = placed[:, None] == slots[None, :]
    chosen_all = jnp.sum(jnp.where(match_block[None, :, :, None, None], chosen[:, None], 0), axis=2)
    before = chosen_all < placed[None, :, None, None]
    mapped_all = jnp.sum(jnp.where(chosen_all[..., None] == slots, slot_of, 0), axis=-1)
    own_slot = slots[None, :, None, None]
    mapped_all = jnp.where(before, mapped_all, own_slot)
    lead_all = jnp.broadcast_to(own_slot, mapped_all.shape[:3] + (1,))
    picks_all = jnp.concatenate([lead_all, mapped_all], axis=-1)
    picks_all = jnp.transpose(
        picks_all.reshape(seqs, nblk, parts_per, hpd, kinds), (1, 2, 0, 3, 4)
    ).reshape(n_ctx, seqs, hpd, kinds)
    dest_group = (jnp.arange(n_ctx, dtype=jnp.int32) % parts_per)[:, None, None, None, None]
    part_ids = jnp.arange(parts_per, dtype=jnp.int32)[None, None, None, None, :]
    route = (picks_all[..., None] * parts_per + part_ids) * parts_per + dest_group
    outgoing = held[seq_ix, head_ix, route]
    fetched = lax.all_to_all(outgoing, "ctx", split_axis=0, concat_axis=0, tiled=True)
    tiles_items = jnp.transpose(fetched, (1, 2, 3, 4, 0, 5)).reshape(
        items, kinds, parts_per * unit, 2 * width
    )
    query_heads = jnp.transpose(query.reshape(seqs, block, hpd, width), (0, 2, 1, 3)).reshape(
        items, block, width
    )
    grad_heads = jnp.transpose(grad_out.reshape(seqs, block, hpd, width), (0, 2, 1, 3)).reshape(
        items, block, width
    )
    sink_items = jnp.tile(sink_mine, seqs)

    def per_head(item):
        q_rows, g_rows, tiles, use_row, sink_logit = item
        return attend_block(q_rows, g_rows, tiles, use_row, sink_logit)

    atts, grads_q, tiles_grad, sink_grads = lax.map(
        per_head, (query_heads, grad_heads, tiles_items, usable.reshape(items, -1), sink_items)
    )
    attended = jnp.transpose(atts.reshape(seqs, hpd, block, width), (0, 2, 1, 3)).reshape(
        seqs, 1, 1, block, hpd * width
    )
    grad_query = jnp.transpose(grads_q.reshape(seqs, hpd, block, width), (0, 2, 1, 3)).reshape(
        seqs, 1, 1, block, hpd * width
    )
    shards = tiles_grad.reshape(seqs, hpd, kinds, parts_per, n_ctx, frag)
    sendback = jnp.transpose(shards, (4, 0, 1, 2, 3, 5))
    landed = lax.all_to_all(sendback, "ctx", split_axis=0, concat_axis=0, tiled=True)
    pooled = (
        jnp.zeros((seqs, hpd, n_ctx * parts_per, frag), jnp.float32)
        .at[seq_ix, head_ix, route]
        .add(landed.astype(jnp.float32))
    )
    pooled = jnp.transpose(pooled.reshape(seqs, hpd, n_ctx, parts_per, frag), (2, 3, 0, 1, 4))
    homed = lax.all_to_all(
        pooled.astype(jnp.bfloat16), "ctx", split_axis=0, concat_axis=0, tiled=True
    ).astype(pooled.dtype)
    totals = jnp.transpose(homed, (1, 2, 3, 0, 4)).reshape(parts_per, seqs, hpd, unit, 2 * width)
    totals = jnp.transpose(totals, (1, 3, 0, 2, 4))
    grad_key = totals[..., :width].reshape(seqs, unit, parts_per * hpd * width).astype(jnp.bfloat16)
    grad_value = (
        totals[..., width:].reshape(seqs, unit, parts_per * hpd * width).astype(jnp.bfloat16)
    )
    sink_local = jnp.sum(sink_grads.reshape(seqs, hpd), axis=0)
    start = lax.axis_index("head") * (parts_per * hpd) + position * hpd
    spread_sink = lax.dynamic_update_slice(jnp.zeros((HEADS,), jnp.float32), sink_local, (start,))
    grad_sink = lax.psum(spread_sink, ("dp", "ctx", "head"))
    return (attended, grad_query, grad_key, grad_value, grad_sink)


def solution(mesh):
    in_specs = (
        P("dp", "ctx", "head", None, None),
        P("dp", "ctx", "head"),
        P("dp", "ctx", "head"),
        P("dp", "ctx", "head", None, None),
        P("dp", None, "head", None),
        P(),
        P("head"),
    )
    out_specs = (
        P("dp", "ctx", "head", None, None),
        P("dp", "ctx", "head", None, None),
        P("dp", "ctx", "head"),
        P("dp", "ctx", "head"),
        P(),
    )
    return jax.shard_map(body, mesh=mesh, in_specs=in_specs, out_specs=out_specs, check_vma=False)
```

profile of v0, /device:TPU:1, one launch (start us, length us, event | category | flops | bytes accessed | tf_op | source)
XLA Modules:
  0.0 485.5 jit_solution(11513940544076405673)
XLA Ops:
  3.3 1.3 copy.152
  4.6 19.1 %all-to-all-start = ((bf16[64,4,1,2,512]{4,3,1,2,0:T(2,128)(2,1)}), bf16[64,4,1,2,512]{4,3,1,2,0:T(2,128)(2,1)S(1)}, u32[]{:S(2)}, u32[]{:S(2)}) async-start(bf16[64,4,1,2,512]{4,3,1,2,0:T(2,128)(2,1)} %copy.152), calls=%async_computation | async-start | bytes 1048576 | tf_op jit(solution)/shard_map/all_to_all | solution.py:92
  27.1 26.0 %all-to-all-done = bf16[64,4,1,2,512]{4,3,1,2,0:T(2,128)(2,1)S(1)} async-done(((bf16[64,4,1,2,512]{4,3,1,2,0:T(2,128)(2,1)}), bf16[64,4,1,2,512]{4,3,1,2,0:T(2,128)(2,1)S(1)}, u32[]{:S(2)}, u32[]{:S(2)}) %all-to-all-start) | async-done | bytes 524320 | tf_op jit(solution)/shard_map/all_to_all | solution.py:92
  53.2 14.1 %gather_fusion = bf16[2048,512]{1,0:T(8,128)(2,1)S(1)} fusion(bf16[1,2,256,512]{3,2,1,0:T(8,128)(2,1)S(1)} %copy.174, s32[2048]{0:T(1024)S(1)} %reshape.369), kind=kCustom, calls=%fused_computation | custom fusion | bytes 4218880 | tf_op jit(solution)/shard_map/gather | solution.py:108
  67.3 2.1 reshape.368
  69.4 9.0 %all-to-all-start.1 = ((bf16[64,1,2,4,4,512]{5,4,3,2,1,0:T(4,128)(2,1)}), bf16[64,1,2,4,4,512]{5,4,3,2,1,0:T(4,128)(2,1)S(1)}, u32[]{:S(2)}, u32[]{:S(2)}) async-start(bf16[64,1,2,4,4,512]{5,4,3,2,1,0:T(4,128)(2,1)} %bitcast.145), calls=%async_computation.1 | async-start | bytes 4194304 | tf_op jit(solution)/shard_map/all_to_all | solution.py:109
  82.3 86.9 %all-to-all-done.1 = bf16[64,1,2,4,4,512]{5,4,3,2,1,0:T(4,128)(2,1)S(1)} async-done(((bf16[64,1,2,4,4,512]{5,4,3,2,1,0:T(4,128)(2,1)}), bf16[64,1,2,4,4,512]{5,4,3,2,1,0:T(4,128)(2,1)S(1)}, u32[]{:S(2)}, u32[]{:S(2)}) %all-to-all-start.1) | async-done | bytes 2097184 | tf_op jit(solution)/shard_map/all_to_all | solution.py:109
  169.2 2.5 copy.159
  171.7 4.1 reshape.337
  175.8 54.9 %while.18 = (s32[]{:T(128)}, bf16[2,512,128]{2,1,0:T(8,128)(2,1)}, bf16[2,512,128]{2,1,0:T(8,128)(2,1)}, bf16[2,4,512,256]{3,2,1,0:T(8,128)(2,1)}, f32[2]{0:T(12...) while((s32[]{:T(128)}, bf16[2,512,128]{2,1,0:T(8,128)(2,1)}, ...), condition=%wide.region_9.10_spmd, body=%wide.region_4.9_spmd.sunk | while | flops 1629425152 | bytes 86695736 | solution.py:125
  176.5 2.6 select_reduce_fusion.5
  181.4 2.4 fusion.76
  187.3 1.9 copy-done
  189.2 1.4 bitcast_dynamic-update-slice_fusion.2
  192.9 3.3 multiply_convert_fusion.2
  198.5 2.3 constant_dynamic-update-slice_fusion.2
  200.8 2.4 fusion.80
  203.9 2.6 select_reduce_fusion.5
  208.8 2.4 fusion.76
  214.7 1.9 copy-done
  216.6 1.4 bitcast_dynamic-update-slice_fusion.2
  220.4 3.3 multiply_convert_fusion.2
  226.0 2.3 constant_dynamic-update-slice_fusion.2
  228.3 2.4 fusion.80
  230.7 2.7 reshape.344
  233.4 3.0 copy.167
  236.4 14.6 %all-to-all-start.2 = ((bf16[64,1,2,4,4,512]{5,4,3,2,1,0:T(4,128)(2,1)}), bf16[64,1,2,4,4,512]{5,4,3,2,1,0:T(4,128)(2,1)S(1)}, u32[]{:S(2)}, u32[]{:S(2)}) async-start(bf16[64,1,2,4,4,512]{5,4,3,2,1,0:T(4,128)(2,1)} %copy.167), calls=%async_computation.2 | async-start | bytes 4194304 | tf_op jit(solution)/shard_map/all_to_all | solution.py:136
  251.5 91.0 %all-to-all-done.2 = bf16[64,1,2,4,4,512]{5,4,3,2,1,0:T(4,128)(2,1)S(1)} async-done(((bf16[64,1,2,4,4,512]{5,4,3,2,1,0:T(4,128)(2,1)}), bf16[64,1,2,4,4,512]{5,4,3,2,1,0:T(4,128)(2,1)S(1)}, u32[]{:S(2)}, u32[]{:S(2)}) %all-to-all-start.2) | async-done | bytes 2097184 | tf_op jit(solution)/shard_map/all_to_all | solution.py:136
  342.5 2.5 reshape.379
  345.0 13.5 %scatter_custom_fusion = f32[512,512]{1,0:T(8,128)S(1)} fusion(s32[2048]{0:T(1024)S(1)} %reshape.377, f32[2048,512]{1,0:T(8,128)} %reshape.379, f32[]{:T(128)} %constant.166.clone.1), kind=kCustom, calls=%fused_computation.55 | custom fusion | flops 1048576 | bytes 1049088
  359.7 13.9 %all-to-all-start.3 = ((bf16[64,4,1,2,512]{4,1,3,2,0:T(4,128)(2,1)}), bf16[64,4,1,2,512]{4,1,3,2,0:T(4,128)(2,1)S(1)}, u32[]{:S(2)}, u32[]{:S(2)}) async-start(bf16[64,4,1,2,512]{4,1,3,2,0:T(4,128)(2,1)} %copy.168), calls=%async_computation.3 | async-start | bytes 1048576 | tf_op jit(solution)/shard_map/all_to_all | solution.py:143
  373.8 105.9 %psum.7 = f32[32]{0:T(128)} all-reduce(f32[32]{0:T(128)S(1)} %dynamic_update_slice.30), channel_id=1, replica_groups=mesh['dp'=2,'ctx'=64,'head'=4] {'dp','ctx','head'}, use_global_device_ids=true, to_apply=%region_11.12 | all-reduce | flops 32 | bytes 256 | tf_op jit(solution)/shard_map/psum | solution.py:155
  (134 shorter events, 36.5 us)
Async XLA Ops:
  0.6 25.9 %copy-start.10 = (s32[3]{0:T(128)S(1)}, s32[3]{0:T(128)}, u32[]{:S(2)}) copy-start(s32[3]{0:T(128)} %constant.189) | copy-start | bytes 40
  0.6 23.1 %copy-start.8 = (s32[16]{0:T(128)S(1)}, s32[16]{0:T(128)}, u32[]{:S(2)}) copy-start(s32[16]{0:T(128)} %param.14) | copy-start | bytes 196
  0.7 23.2 %copy-start.7 = (s32[1,16,8,3]{1,2,3,0:T(8,128)S(1)}, s32[1,16,8,3]{1,2,3,0:T(8,128)}, u32[]{:S(2)}) copy-start(s32[1,16,8,3]{1,2,3,0:T(8,128)} %param.13) | copy-start | bytes 4612
  4.6 48.5 %all-to-all-start = ((bf16[64,4,1,2,512]{4,3,1,2,0:T(2,128)(2,1)}), bf16[64,4,1,2,512]{4,3,1,2,0:T(2,128)(2,1)S(1)}, u32[]{:S(2)}, u32[]{:S(2)}) async-start(bf16[64,4,1,2,512]{4,3,1,2,0:T(2,128)(2,1)} %copy.152), calls=%async_computation | async-start | bytes 1048576 | tf_op jit(solution)/shard_map/all_to_all | solution.py:92
  67.3 13.9 %copy-start.11 = (f32[8]{0:T(128)S(1)}, f32[8]{0:T(128)}, u32[]{:S(2)}) copy-start(f32[8]{0:T(128)} %param.15) | copy-start | bytes 100
  67.3 14.0 %copy-start.4 = (bf16[1,1,1,512,256]{4,3,2,1,0:T(8,128)(2,1)S(1)}, bf16[1,1,1,512,256]{4,3,2,1,0:T(8,128)(2,1)}, u32[]{:S(2)}) copy-start(bf16[1,1,1,512,256]{4,3,2,1,0:T(8,128)(2,1)} %param.9) | copy-start | bytes 786436
  69.4 12.0 %copy-start.5 = (bf16[1,1,1,512,256]{4,3,2,1,0:T(8,128)(2,1)S(1)}, bf16[1,1,1,512,256]{4,3,2,1,0:T(8,128)(2,1)}, u32[]{:S(2)}) copy-start(bf16[1,1,1,512,256]{4,3,2,1,0:T(8,128)(2,1)} %param.12) | copy-start | bytes 786436
  69.4 99.8 %all-to-all-start.1 = ((bf16[64,1,2,4,4,512]{5,4,3,2,1,0:T(4,128)(2,1)}), bf16[64,1,2,4,4,512]{5,4,3,2,1,0:T(4,128)(2,1)S(1)}, u32[]{:S(2)}, u32[]{:S(2)}) async-start(bf16[64,1,2,4,4,512]{5,4,3,2,1,0:T(4,128)(2,1)} %bitcast.145), calls=%async_computation.1 | async-start | bytes 4194304 | tf_op jit(solution)/shard_map/all_to_all | solution.py:109
  175.8 14.8 %copy-start.2 = (bf16[2,512,128]{1,2,0:T(8,128)(2,1)}, bf16[2,512,128]{1,2,0:T(8,128)(2,1)S(1)}, u32[]{:S(2)}) copy-start(bf16[2,512,128]{1,2,0:T(8,128)(2,1)S(1)} %get-tuple-element.386) | copy-start | bytes 786436 | tf_op jit(solution)/shard_map/while
  187.2 1.9 copy-start
  192.9 3.7 copy-start.1
  198.5 4.7 copy-start.3
  203.2 14.8 %copy-start.2 = (bf16[2,512,128]{1,2,0:T(8,128)(2,1)}, bf16[2,512,128]{1,2,0:T(8,128)(2,1)S(1)}, u32[]{:S(2)}) copy-start(bf16[2,512,128]{1,2,0:T(8,128)(2,1)S(1)} %get-tuple-element.386) | copy-start | bytes 786436 | tf_op jit(solution)/shard_map/while
  214.7 1.9 copy-start
  220.4 3.7 copy-start.1
  226.0 4.7 copy-start.3
  233.4 17.6 %copy-start.9 = (s32[3]{0:T(128)S(1)}, s32[3]{0:T(128)}, u32[]{:S(2)}) copy-start(s32[3]{0:T(128)} %constant.192) | copy-start | bytes 40
  236.4 106.2 %all-to-all-start.2 = ((bf16[64,1,2,4,4,512]{5,4,3,2,1,0:T(4,128)(2,1)}), bf16[64,1,2,4,4,512]{5,4,3,2,1,0:T(4,128)(2,1)S(1)}, u32[]{:S(2)}, u32[]{:S(2)}) async-start(bf16[64,1,2,4,4,512]{5,4,3,2,1,0:T(4,128)(2,1)} %copy.167), calls=%async_computation.2 | async-start | bytes 4194304 | tf_op jit(solution)/shard_map/all_to_all | solution.py:136
  345.0 136.8 %copy-start.6 = (bf16[2,512,128]{2,1,0:T(8,128)(2,1)S(1)}, bf16[2,512,128]{2,1,0:T(8,128)(2,1)}, u32[]{:S(2)}) copy-start(bf16[2,512,128]{2,1,0:T(8,128)(2,1)} %get-tuple-element.137) | copy-start | bytes 786436
  359.7 123.3 %all-to-all-start.3 = ((bf16[64,4,1,2,512]{4,1,3,2,0:T(4,128)(2,1)}), bf16[64,4,1,2,512]{4,1,3,2,0:T(4,128)(2,1)S(1)}, u32[]{:S(2)}, u32[]{:S(2)}) async-start(bf16[64,4,1,2,512]{4,1,3,2,0:T(4,128)(2,1)} %copy.168), calls=%async_computation.3 | async-start | bytes 1048576 | tf_op jit(solution)/shard_map/all_to_all | solution.py:143
where the time goes:
time: 487 us; the launch traced here: 486 us
  waiting for transfers between devices  204 us (42%)
  blocking collectives  106 us (22%)
  local copies, waits for them, and re-layouts  62.7 us (13%)
  starting transfers between devices  56.5 us (12%)
  other arithmetic  31.3 us (6%)
  matrix products  20.7 us (4%)
    psum x1, blocking collectives, body(): grad_sink = lax.psum(spread_sink, ('dp', 'ctx', 'head'))  106 us
    all_to_all x1, waiting for transfers between devices, body(): lax.all_to_all(sendback, 'ctx', split_axis=0, concat_axis=0, tiled=True)  91 us
    all_to_all x1, waiting for transfers between devices, body(): lax.all_to_all(outgoing, 'ctx', split_axis=0, concat_axis=0, tiled=True)  86.9 us
    all_to_all x1, waiting for transfers between devices, body(): lax.all_to_all(spread, 'ctx', split_axis=0, concat_axis=0, tiled=True)  26 us
    all_to_all x1, starting transfers between devices, body(): lax.all_to_all(spread, 'ctx', split_axis=0, concat_axis=0, tiled=True)  19.1 us
    gather x2, local copies, waits for them, and re-layouts, body(): outgoing = held[seq_ix, head_ix, route]  16.2 us
    all_to_all x1, starting transfers between devices, body(): lax.all_to_all(sendback, 'ctx', split_axis=0, concat_axis=0, tiled=True)  14.6 us
    all_to_all x1, starting transfers between devices, body(): lax.all_to_all(pooled.astype(jnp.bfloat16), 'ctx', split_axis=0, concat_a...  13.9 us
  transfers between devices with their start and end apart: 4, of which 3 were waited for; matrix products, arithmetic and copies ran while one was open for 2% of the time, Pallas kernels for 0%

commit v1 on v0

--- a/solution.py
+++ b/solution.py
@@ -152,7 +152,7 @@
     sink_local = jnp.sum(sink_grads.reshape(seqs, hpd), axis=0)
     start = lax.axis_index("head") * (parts_per * hpd) + position * hpd
     spread_sink = lax.dynamic_update_slice(jnp.zeros((HEADS,), jnp.float32), sink_local, (start,))
-    grad_sink = lax.psum(spread_sink, ("dp", "ctx", "head"))
+    grad_sink = jnp.sum(lax.all_gather(spread_sink, ("dp", "ctx", "head")), axis=0)
     return (attended, grad_query, grad_key, grad_value, grad_sink)
 
 

time: 487 us -> 1630 us (3.35)
  blocking collectives: 106 us -> 1250 us
    all_gather x0 -> x1, blocking collectives: none -> 1250 us  [body(): lax.all_gather(spread_sink, ('dp', 'ctx', 'head'))]
    psum x1 -> x0, blocking collectives: 106 us -> none  [body(): grad_sink = lax.psum(spread_sink, ('dp', 'ctx', 'head'))]
  transfers between devices with their start and end apart: 4 -> 4, of which waited for: 3 -> 3; matrix products, arithmetic and copies ran while one was open for 2% -> 1% of each run, Pallas kernels for 0% -> 0%
where the time goes in v1:
time: 1630 us
  blocking collectives  1250 us (77%)
  waiting for transfers between devices  204 us (13%)
  local copies, waits for them, and re-layouts  62.6 us (4%)
  starting transfers between devices  56.5 us (3%)
  other arithmetic  32.4 us (2%)
  matrix products  20.7 us (1%)
    all_gather x1, blocking collectives, body(): lax.all_gather(spread_sink, ('dp', 'ctx', 'head'))  1250 us
    all_to_all x1, waiting for transfers between devices, body(): lax.all_to_all(sendback, 'ctx', split_axis=0, concat_axis=0, tiled=True)  91 us
    all_to_all x1, waiting for transfers between devices, body(): lax.all_to_all(outgoing, 'ctx', split_axis=0, concat_axis=0, tiled=True)  86.9 us
  transfers between devices with their start and end apart: 4, of which 3 were waited for; matrix products, arithmetic and copies ran while one was open for 1% of the time, Pallas kernels for 0%

profile of v1, /device:TPU:1, one launch (start us, length us, event | category | flops | bytes accessed | tf_op | source)
XLA Modules:
  0.0 1627.4 jit_solution(2943128888998168485)
XLA Ops:
  3.3 1.3 copy.152
  4.6 19.1 %all-to-all-start = ((bf16[64,4,1,2,512]{4,3,1,2,0:T(2,128)(2,1)}), bf16[64,4,1,2,512]{4,3,1,2,0:T(2,128)(2,1)S(1)}, u32[]{:S(2)}, u32[]{:S(2)}) async-start(bf16[64,4,1,2,512]{4,3,1,2,0:T(2,128)(2,1)} %copy.152), calls=%async_computation | async-start | bytes 1048576 | tf_op jit(solution)/shard_map/all_to_all | solution.py:92
  27.1 26.0 %all-to-all-done = bf16[64,4,1,2,512]{4,3,1,2,0:T(2,128)(2,1)S(1)} async-done(((bf16[64,4,1,2,512]{4,3,1,2,0:T(2,128)(2,1)}), bf16[64,4,1,2,512]{4,3,1,2,0:T(2,128)(2,1)S(1)}, u32[]{:S(2)}, u32[]{:S(2)}) %all-to-all-start) | async-done | bytes 524320 | tf_op jit(solution)/shard_map/all_to_all | solution.py:92
  53.2 14.1 gather_fusion
  67.3 2.1 reshape.371
  69.4 9.0 all-to-all-start.1
  82.3 86.9 %all-to-all-done.1 = bf16[64,1,2,4,4,512]{5,4,3,2,1,0:T(4,128)(2,1)S(1)} async-done(((bf16[64,1,2,4,4,512]{5,4,3,2,1,0:T(4,128)(2,1)}), bf16[64,1,2,4,4,512]{5,4,3,2,1,0:T(4,128)(2,1)S(1)}, u32[]{:S(2)}, u32[]{:S(2)}) %all-to-all-start.1) | async-done | bytes 2097184 | tf_op jit(solution)/shard_map/all_to_all | solution.py:109
  169.2 2.5 copy.159
  171.7 4.1 reshape.340
  175.8 54.9 %while.18 = (s32[]{:T(128)}, bf16[2,512,128]{2,1,0:T(8,128)(2,1)}, bf16[2,512,128]{2,1,0:T(8,128)(2,1)}, bf16[2,4,512,256]{3,2,1,0:T(8,128)(2,1)}, f32[2]{0:T(12...) while((s32[]{:T(128)}, bf16[2,512,128]{2,1,0:T(8,128)(2,1)}, ...), condition=%wide.region_9.10_spmd, body=%wide.region_4.9_spmd.sunk | while | flops 1629425152 | bytes 86695736 | solution.py:125
  176.5 2.6 select_reduce_fusion.5
  181.4 2.4 fusion.76
  187.3 1.9 copy-done
  189.2 1.4 bitcast_dynamic-update-slice_fusion.2
  192.9 3.3 multiply_convert_fusion.2
  198.5 2.3 constant_dynamic-update-slice_fusion.2
  200.8 2.4 fusion.80
  203.9 2.6 select_reduce_fusion.5
  208.8 2.4 fusion.76
  214.7 1.9 copy-done
  216.6 1.4 bitcast_dynamic-update-slice_fusion.2
  220.4 3.3 multiply_convert_fusion.2
  226.0 2.3 constant_dynamic-update-slice_fusion.2
  228.3 2.4 fusion.80
  230.7 2.7 reshape.347
  233.4 3.0 copy.167
  236.4 14.6 all-to-all-start.2
  251.5 91.0 %all-to-all-done.2 = bf16[64,1,2,4,4,512]{5,4,3,2,1,0:T(4,128)(2,1)S(1)} async-done(((bf16[64,1,2,4,4,512]{5,4,3,2,1,0:T(4,128)(2,1)}), bf16[64,1,2,4,4,512]{5,4,3,2,1,0:T(4,128)(2,1)S(1)}, u32[]{:S(2)}, u32[]{:S(2)}) %all-to-all-start.2) | async-done | bytes 2097184 | tf_op jit(solution)/shard_map/all_to_all | solution.py:136
  342.5 2.5 reshape.382
  345.0 13.5 scatter_custom_fusion
  359.7 13.9 all-to-all-start.3
  376.9 1246.9 %all-gather = f32[512,1,32]{2,1,0:T(1,128)S(1)} all-gather(f32[1,1,32]{2,1,0:T(1,128)S(1)} %dynamic_update_slice.32), channel_id=1, replica_groups=mesh['dp'=2,'ctx'=64,'head'=4] {'dp','ctx','head'}, dimensions={0}, use_global_device_ids=true | all-gather | bytes 65664 | tf_op jit(solution)/shard_map/all_gather | solution.py:155
  (135 shorter events, 37.4 us)
Async XLA Ops:
  0.6 25.9 %copy-start.10 = (s32[3]{0:T(128)S(1)}, s32[3]{0:T(128)}, u32[]{:S(2)}) copy-start(s32[3]{0:T(128)} %constant.190) | copy-start | bytes 40
  0.6 23.1 %copy-start.8 = (s32[16]{0:T(128)S(1)}, s32[16]{0:T(128)}, u32[]{:S(2)}) copy-start(s32[16]{0:T(128)} %param.14) | copy-start | bytes 196
  0.7 23.2 %copy-start.7 = (s32[1,16,8,3]{1,2,3,0:T(8,128)S(1)}, s32[1,16,8,3]{1,2,3,0:T(8,128)}, u32[]{:S(2)}) copy-start(s32[1,16,8,3]{1,2,3,0:T(8,128)} %param.13) | copy-start | bytes 4612
  4.6 48.5 %all-to-all-start = ((bf16[64,4,1,2,512]{4,3,1,2,0:T(2,128)(2,1)}), bf16[64,4,1,2,512]{4,3,1,2,0:T(2,128)(2,1)S(1)}, u32[]{:S(2)}, u32[]{:S(2)}) async-start(bf16[64,4,1,2,512]{4,3,1,2,0:T(2,128)(2,1)} %copy.152), calls=%async_computation | async-start | bytes 1048576 | tf_op jit(solution)/shard_map/all_to_all | solution.py:92
  67.3 13.9 copy-start.11
  67.3 14.0 copy-start.4
  69.4 12.0 copy-start.5
  69.4 99.8 %all-to-all-start.1 = ((bf16[64,1,2,4,4,512]{5,4,3,2,1,0:T(4,128)(2,1)}), bf16[64,1,2,4,4,512]{5,4,3,2,1,0:T(4,128)(2,1)S(1)}, u32[]{:S(2)}, u32[]{:S(2)}) async-start(bf16[64,1,2,4,4,512]{5,4,3,2,1,0:T(4,128)(2,1)} %bitcast.146), calls=%async_computation.1 | async-start | bytes 4194304 | tf_op jit(solution)/shard_map/all_to_all | solution.py:109
  175.8 14.8 copy-start.2
  187.2 1.9 copy-start
  192.9 3.7 copy-start.1
  198.5 4.7 copy-start.3
  203.2 14.8 copy-start.2
  214.7 1.9 copy-start
  220.4 3.7 copy-start.1
  226.0 4.7 copy-start.3
  233.4 17.6 %copy-start.9 = (s32[3]{0:T(128)S(1)}, s32[3]{0:T(128)}, u32[]{:S(2)}) copy-start(s32[3]{0:T(128)} %constant.193) | copy-start | bytes 40
  236.4 106.2 %all-to-all-start.2 = ((bf16[64,1,2,4,4,512]{5,4,3,2,1,0:T(4,128)(2,1)}), bf16[64,1,2,4,4,512]{5,4,3,2,1,0:T(4,128)(2,1)S(1)}, u32[]{:S(2)}, u32[]{:S(2)}) async-start(bf16[64,1,2,4,4,512]{5,4,3,2,1,0:T(4,128)(2,1)} %copy.167), calls=%async_computation.2 | async-start | bytes 4194304 | tf_op jit(solution)/shard_map/all_to_all | solution.py:136
  345.0 30.7 %copy-start.6 = (bf16[2,512,128]{2,1,0:T(8,128)(2,1)S(1)}, bf16[2,512,128]{2,1,0:T(8,128)(2,1)}, u32[]{:S(2)}) copy-start(bf16[2,512,128]{2,1,0:T(8,128)(2,1)} %get-tuple-element.137) | copy-start | bytes 786436
  359.7 1265.1 %all-to-all-start.3 = ((bf16[64,4,1,2,512]{4,1,3,2,0:T(4,128)(2,1)}), bf16[64,4,1,2,512]{4,1,3,2,0:T(4,128)(2,1)S(1)}, u32[]{:S(2)}, u32[]{:S(2)}) async-start(bf16[64,4,1,2,512]{4,1,3,2,0:T(4,128)(2,1)} %copy.168), calls=%async_computation.3 | async-start | bytes 1048576 | tf_op jit(solution)/shard_map/all_to_all | solution.py:143
